TPU v7x, 128 devices: a whole 4x4x4 slice. The times are simulated.
128 devices in a mesh: dp: 8 (over y_lo, x), mp: 16 (over y_hi, z, core).
Axes of the slice: x: 4, y: 4 (y_hi: 2, y_lo: 2; y = y_hi * 2 + y_lo), z: 4, core: 2. Of those that a mesh axis runs over, the one named last changes fastest.
Arguments:
- tokens: bfloat16 [16384, 2304], P(('dp', 'mp')), may hold values from -6 to 6
- ada_ffn: float32 [16, 2, 2304], P('dp'), may hold values from -4 to 4
- ffn_gate: float32 [16, 2304], P('dp'), may hold values from 0.5 to 1.5
- up_weight: bfloat16 [2304, 9216], P(None, 'mp'), may hold values from -0.125 to 0.125
- up_bias: float32 [9216], P('mp'), may hold values from -6 to 6
- down_weight: bfloat16 [9216, 2304], P('mp'), may hold values from -0.125 to 0.125
- down_bias: float32 [2304], replicated, may hold values from -6 to 6
- ada_head: float32 [16, 2, 2304], P('dp'), may hold values from -4 to 4
- head_weight: bfloat16 [2304, 4096], P(None, 'mp'), may hold values from -0.125 to 0.125
- head_bias: float32 [4096], P('mp'), may hold values from -6 to 6
- gumbel_noise: float32 [8, 1024, 4096], P('dp', None, 'mp'), as said below
- codebook: bfloat16 [4096, 32], P('mp'), may hold values from -16 to 16
- phi_weight: float32 [32, 32, 3, 3], replicated, may hold values from -0.375 to 0.375
- phi_bias: float32 [32], replicated, may hold values from -6 to 6
- f_hat: float32 [8, 32, 1024], P('dp', None, 'mp'), may hold values from -6 to 6
Outputs:
- block_out: bfloat16 [16384, 2304], P(('dp', 'mp'))
- f_hat_out: float32 [8, 32, 1024], P('dp', None, 'mp')
Inputs may be any that keep to these rules, and one draw needn't show every extreme that they name: `gumbel_noise`: noise added to the guided logits.
All inputs are finite; a program needn't handle non-finite values.
Results may differ from a plain program's by a relative error of at most 0.024.
Values may be sent and summed in bfloat16 or wider, within the bound.
A program may use at most 256 MiB of HBM per device.

v0:
```python
import jax
import jax.numpy as jnp
from jax import lax
from jax.sharding import PartitionSpec as P

SIDE = 32
NEW = 1024
GUIDE = 1.5


def from_partner(value, axis, apart):
    mask = 2**apart
    pairs = [(source, source ^ mask) for source in range(lax.axis_size(axis))]
    return lax.ppermute(value, axis, pairs)


def norm_rows(values):
    row_mean = jnp.mean(values, axis=-1, keepdims=True)
    centred = values - row_mean
    spread = jnp.mean(centred * centred, axis=-1, keepdims=True)
    return centred * lax.rsqrt(spread + 1e-06)


def per_image(lookup, row_images):
    picked = jnp.broadcast_to(lookup[0], (row_images.shape[0],) + lookup.shape[1:])
    chosen = (row_images == 1).reshape((-1,) + (1,) * (lookup.ndim - 1))
    picked = jnp.where(chosen, lookup[1], picked)
    return picked


def modulate(values, ada_rows):
    return (norm_rows(values) * (1.0 + ada_rows[:, 1]) + ada_rows[:, 0]).astype(jnp.bfloat16)


def body(
    tokens,
    ada_ffn,
    ffn_gate,
    up_weight,
    up_bias,
    down_weight,
    down_bias,
    ada_head,
    head_weight,
    head_bias,
    gumbel_noise,
    codebook,
    phi_weight,
    phi_bias,
    f_hat,
):
    row_count = tokens.shape[0]
    shard_count = lax.axis_size("mp")
    mp_index = lax.axis_index("mp")
    group_rows = row_count * shard_count
    own_images = (mp_index * row_count + jnp.arange(row_count, dtype=jnp.int32)) // NEW
    gathered = lax.all_gather(tokens, "mp", axis=0, tiled=True)
    row_images = jnp.arange(group_rows, dtype=jnp.int32) // NEW
    full_hidden = jax.nn.gelu(
        jnp.dot(
            modulate(gathered.astype(jnp.float32), per_image(ada_ffn, row_images)),
            up_weight,
            preferred_element_type=jnp.float32,
        )
        + up_bias,
        approximate=True,
    ).astype(jnp.bfloat16)
    summed = lax.psum_scatter(
        jnp.dot(full_hidden, down_weight, preferred_element_type=jnp.float32),
        "mp",
        scatter_dimension=0,
        tiled=True,
    )
    block_out = (
        tokens.astype(jnp.float32) + per_image(ffn_gate, own_images) * (summed + down_bias)
    ).astype(jnp.bfloat16)
    full_out = lax.all_gather(block_out, "mp", axis=0, tiled=True)
    logits = (
        jnp.dot(
            modulate(full_out.astype(jnp.float32), per_image(ada_head, row_images)),
            head_weight,
            preferred_element_type=jnp.float32,
        )
        + head_bias
    )
    half_rows = group_rows // 2
    upper_half = lax.axis_index("dp") // (lax.axis_size("dp") // 2)
    kept_rows = lax.dynamic_slice_in_dim(logits, upper_half * half_rows, half_rows, 0)
    sent_rows = lax.dynamic_slice_in_dim(logits, (1 - upper_half) * half_rows, half_rows, 0)
    twin_rows = from_partner(sent_rows, "dp", lax.axis_size("dp").bit_length() - 2)
    cond_rows = jnp.where(upper_half == 0, kept_rows, twin_rows)
    uncond_rows = jnp.where(upper_half == 0, twin_rows, kept_rows)
    scores = (1.0 + GUIDE) * cond_rows - GUIDE * uncond_rows + gumbel_noise.reshape(half_rows, -1)
    row_peak = jnp.max(scores, axis=1)
    weights = jnp.exp(scores - row_peak[:, None]).astype(jnp.bfloat16)
    row_total = jnp.sum(weights.astype(jnp.float32), axis=1)
    mixed_code = jnp.dot(weights, codebook, preferred_element_type=jnp.float32)
    global_peak = lax.pmax(row_peak, "mp")
    factor = jnp.exp(row_peak - global_peak)
    row_total, mixed_code = (
        lax.psum((row_total * factor).astype(jnp.bfloat16), "mp").astype(jnp.float32),
        lax.psum((mixed_code * factor[:, None]).astype(jnp.bfloat16), "mp").astype(jnp.float32),
    )
    soft_code = mixed_code / row_total[:, None]
    pair_count = f_hat.shape[0]
    channels = f_hat.shape[1]
    band_rows = f_hat.shape[2] // SIDE
    code_maps = soft_code.reshape(pair_count, SIDE, SIDE, channels)
    padded = jnp.pad(code_maps, ((0, 0), (1, 1), (1, 1), (0, 0)))
    window = lax.dynamic_slice_in_dim(padded, mp_index * band_rows, band_rows + 2, 1)
    conv_out = (
        jnp.zeros((pair_count, channels, band_rows, SIDE), jnp.float32)
        + phi_bias[None, :, None, None]
    )
    for row_step in range(3):
        for col_step in range(3):
            conv_out = conv_out + jnp.einsum(
                "pyxc,oc->poyx",
                window[:, row_step : row_step + band_rows, col_step : col_step + SIDE, :],
                phi_weight[:, :, row_step, col_step],
                precision=lax.Precision.HIGHEST,
            )
    own_cells = jnp.transpose(window[:, 1 : band_rows + 1, 1 : SIDE + 1, :], (0, 3, 1, 2))
    f_hat_out = f_hat + (0.5 * own_cells + 0.5 * conv_out).reshape(
        pair_count, channels, band_rows * SIDE
    )
    return (block_out, f_hat_out)


def solution(mesh):
    in_specs = (
        P(("dp", "mp"), None),
        P("dp", None, None),
        P("dp", None),
        P(None, "mp"),
        P("mp"),
        P("mp", None),
        P(),
        P("dp", None, None),
        P(None, "mp"),
        P("mp"),
        P("dp", None, "mp"),
        P("mp", None),
        P(),
        P(),
        P("dp", None, "mp"),
    )
    out_specs = (P(("dp", "mp"), None), P("dp", None, "mp"))
    return jax.shard_map(body, mesh=mesh, in_specs=in_specs, out_specs=out_specs, check_vma=False)
```

profile of v0, /device:TPU:0, one launch (start us, length us, event | category | flops | bytes accessed | tf_op | source)
XLA Modules:
  0.0 590.4 jit_solution(9555418837395056854)
XLA Ops:
  7.2 0.7 all-gather.3.cloned.1.call-update
  8.0 0.8 slice_bitcast_fusion.3
  8.8 24.7 %broadcast_select_fusion = (f32[2048,2,2304]{2,0,1:T(8,128)}, f32[2048,2,2304]{2,0,1:T(8,128)}) fusion(f32[2,2304]{1,0:T(2,128)S(1)} %get-tuple-element.9, f32[2,2304]{1,0:T(2,128)S(1)} %get-tuple-element.8, pred[2048]{0:T(1024)(128)(4,1)S(1)} %fusion.70, f32[2,2304]{1,0:T(2,128)S(1)} %get-tuple-element.14, f32[2,2304]{1,0:T(2,128)S(1)} %get-tuple-element.15), kind=kLoop, calls=%fused_computation.22 | loop fusion | flops 18874368 | bytes 75573248 | tf_op jit(solution)/shard_map/jit(_where)/select_n | solution.py:27
  33.4 57.1 %all-gather.3.cloned.1.call-done = bf16[2048,2304]{1,0:T(8,128)(2,1)} async-done(((bf16[128,2304]{1,0:T(8,128)(2,1)}), bf16[2048,2304]{1,0:T(8,128)(2,1)}) %all-gather.3.cloned.1.call-update) | async-done | bytes 9437200 | tf_op jit(solution)/shard_map/all_gather | solution.py:57
  90.6 5.1 convert_reduce_fusion.1
  95.7 1.2 copy-done.3
  96.9 2.6 fusion.8
  99.6 28.5 %fusion.29 = f32[2048,2304]{1,0:T(8,128)} fusion(bf16[576,2304]{1,0:T(8,128)(2,1)S(1)} %copy-done, bf16[2304,576]{0,1:T(8,128)(2,1)} %param.18, bf16[2048,2304]{1,0:T(8,128)(2,1)} %all-gather.3.cloned.1.call-done, f32[2048,2,2304]{2,0,1:T(8,128)} %get-tuple-element.13, f32[2048]{0:T(1024)S(1)} %add_rsqrt_fusion.1, f32[2048]{0:T(1024)S(1)} %broadcast_multiply_fusion.1, ...), kind=kOutput, calls=%fused_computation.35 | convolution fusion | flops 10916462592 | bytes 71387392 | tf_op jit(solution)/shard_map/dot_general | solution.py:69
  128.2 0.6 copy-done.7
  128.9 156.1 %reduce-scatter.2.cloned.1.call-done = f32[128,2304]{1,0:T(8,128)} async-done(((f32[2048,2304]{1,0:T(8,128)}), f32[128,2304]{1,0:T(8,128)}) %reduce-scatter.2.cloned.1.call-update) | async-done | bytes 1179664 | tf_op jit(solution)/shard_map/reduce_scatter | solution.py:68
  285.0 2.4 add_convert_fusion
  287.3 0.2 all-reduce.3.cloned.1.call-start
  287.6 75.9 %all-gather.5.cloned.1.call-done = bf16[2048,2304]{1,0:T(8,128)(2,1)} async-done(((bf16[128,2304]{1,0:T(8,128)(2,1)}), bf16[2048,2304]{1,0:T(8,128)(2,1)}) %all-gather.5.cloned.1.call-update) | async-done | bytes 9437200 | tf_op jit(solution)/shard_map/all_gather | solution.py:77
  363.5 5.1 convert_reduce_fusion
  368.6 1.2 copy-done.2
  369.8 2.6 fusion.4
  372.5 14.0 %fusion.31 = f32[2048,256]{0,1:T(8,128)S(1)} fusion(bf16[2304,256]{1,0:T(8,128)(2,1)S(1)} %copy-done.12, bf16[2048,2304]{1,0:T(8,128)(2,1)S(1)} %copy-done.2, f32[2048,2,2304]{2,0,1:T(8,128)} %get-tuple-element.12, f32[2048]{0:T(1024)S(1)} %add_rsqrt_fusion, f32[2048]{0:T(1024)S(1)} %broadcast_multiply_fusion, f32[256]{0:T(256)S(1)} %copy-done.14), kind=kOutput, calls=%fused_computation.36 | convolution fusion | flops 2449473536 | bytes 50480128 | tf_op jit(solution)/shard_map/dot_general | solution.py:79
  386.5 1.3 copy-done.5
  387.8 1.1 constant_dynamic-slice_fusion
  388.9 0.6 collective-permute-start
  389.5 2.5 copy.17
  392.0 22.5 %collective-permute-done = f32[1024,256]{0,1:T(8,128)} collective-permute-done((f32[1024,256]{0,1:T(8,128)}, f32[1024,256]{0,1:T(8,128)}, u32[]{:S(2)}, u32[]{:S(2)}) %collective-permute-start) | collective-permute-done | bytes 1048608 | tf_op jit(solution)/shard_map/ppermute | solution.py:14
  414.5 3.3 fusion.97
  417.8 33.6 %pmax.7 = f32[1024]{0:T(1024)S(1)} all-reduce(f32[1024]{0:T(1024)S(1)} %get-tuple-element.6), channel_id=1, replica_groups=mesh['dp'=8,'mp'=16] {'mp'}, use_global_device_ids=true, to_apply=%region_6.7 | all-reduce | flops 1024 | bytes 8192 | tf_op jit(solution)/shard_map/pmax | solution.py:98
  451.4 1.4 convert_reduce_fusion.2
  452.8 2.1 fusion.39
  454.9 33.2 %psum.15 = bf16[1024]{0:T(1024)(128)(2,1)S(1)} all-reduce(bf16[1024]{0:T(1024)(128)(2,1)S(1)} %get-tuple-element.4), channel_id=1, replica_groups=mesh['dp'=8,'mp'=16] {'mp'}, use_global_device_ids=true, to_apply=%region_9.10 | all-reduce | flops 1024 | bytes 4096 | tf_op jit(solution)/shard_map/psum | solution.py:101
  488.1 92.3 %all-reduce.3.cloned.1.call-done = bf16[1024,32]{0,1:T(8,128)(2,1)} async-done(((bf16[1024,32]{0,1:T(8,128)(2,1)}), bf16[1024,32]{0,1:T(8,128)(2,1)}) %all-reduce.3.cloned.1.call-update) | async-done | bytes 65552 | tf_op jit(solution)/shard_map/psum | solution.py:102
  580.4 0.9 convert_divide_fusion
  581.3 0.2 copy.20
  583.0 0.2 fusion.42
  583.2 0.6 add.204
  (50 shorter events, 1.8 us)
Async XLA Ops:
  7.2 92.4 %copy-start = (bf16[576,2304]{1,0:T(8,128)(2,1)S(1)}, bf16[576,2304]{1,0:T(8,128)(2,1)}, u32[]{:S(2)}) copy-start(bf16[576,2304]{1,0:T(8,128)(2,1)} %param.20) | copy-start | bytes 7962628
  7.2 83.4 %all-gather.3.cloned.1.call-start = ((), (), s32[]{:S(2)}) async-start(), calls=%async_computation.1 | async-start | bytes 10027008 | tf_op jit(solution)/shard_map/all_gather | solution.py:57
  7.9 277.0 %reduce-scatter.2.cloned.1.call-start = ((), (), s32[]{:S(2)}) async-start(), calls=%async_computation.2 | async-start | bytes 20054016 | tf_op jit(solution)/shard_map/reduce_scatter | solution.py:68
  33.4 66.1 %copy-start.13 = (f32[576]{0:T(1024)S(1)}, f32[576]{0:T(1024)}, u32[]{:S(2)}) copy-start(f32[576]{0:T(1024)} %param.19) | copy-start | bytes 6916
  90.6 6.4 %copy-start.3 = (bf16[2048,2304]{1,0:T(8,128)(2,1)S(1)}, bf16[2048,2304]{1,0:T(8,128)(2,1)}, u32[]{:S(2)}) copy-start(bf16[2048,2304]{1,0:T(8,128)(2,1)} %all-gather.3.cloned.1.call-done) | copy-start | bytes 28311556
  128.1 0.7 copy-start.7
  128.1 156.9 %copy-start.4 = (bf16[128,2304]{1,0:T(8,128)(2,1)S(1)}, bf16[128,2304]{1,0:T(8,128)(2,1)}, u32[]{:S(2)}) copy-start(bf16[128,2304]{1,0:T(8,128)(2,1)} %param.15) | copy-start | bytes 1769476
  128.1 156.9 %copy-start.10 = (f32[2304]{0:T(1024)S(1)}, f32[2304]{0:T(1024)}, u32[]{:S(2)}) copy-start(f32[2304]{0:T(1024)} %param.21) | copy-start | bytes 27652
  128.1 235.3 %all-gather.5.cloned.1.call-start = ((), (), s32[]{:S(2)}) async-start(), calls=%async_computation.3 | async-start | bytes 10027008 | tf_op jit(solution)/shard_map/all_gather | solution.py:77
  287.3 293.1 %all-reduce.3.cloned.1.call-start = ((), (), s32[]{:S(2)}) async-start(), calls=%async_computation.4 | async-start | bytes 131072 | tf_op jit(solution)/shard_map/psum | solution.py:102
  287.6 84.8 %copy-start.14 = (f32[256]{0:T(256)S(1)}, f32[256]{0:T(256)}, u32[]{:S(2)}) copy-start(f32[256]{0:T(256)} %param.24) | copy-start | bytes 3076
  363.5 6.4 %copy-start.2 = (bf16[2048,2304]{1,0:T(8,128)(2,1)S(1)}, bf16[2048,2304]{1,0:T(8,128)(2,1)}, u32[]{:S(2)}) copy-start(bf16[2048,2304]{1,0:T(8,128)(2,1)} %all-gather.5.cloned.1.call-done) | copy-start | bytes 28311556
  363.5 9.0 %copy-start.12 = (bf16[2304,256]{1,0:T(8,128)(2,1)S(1)}, bf16[2304,256]{1,0:T(8,128)(2,1)}, u32[]{:S(2)}) copy-start(bf16[2304,256]{1,0:T(8,128)(2,1)} %param.23) | copy-start | bytes 3538948
  372.4 211.4 %copy-start.1 = (bf16[576,2304]{1,0:T(8,128)(2,1)S(1)}, bf16[576,2304]{1,0:T(8,128)(2,1)}, u32[]{:S(2)}) copy-start(bf16[576,2304]{1,0:T(8,128)(2,1)} %param.20) | copy-start | bytes 7962628
  386.5 1.4 copy-start.5
  387.8 64.9 %copy-start.8 = (bf16[256,32]{0,1:T(8,128)(2,1)S(1)}, bf16[256,32]{0,1:T(8,128)(2,1)}, u32[]{:S(2)}) copy-start(bf16[256,32]{0,1:T(8,128)(2,1)} %param.26) | copy-start | bytes 49156
  387.8 193.7 %copy-start.6 = (f32[32,32,3,3]{1,0,3,2:T(8,128)S(1)}, f32[32,32,3,3]{1,0,3,2:T(8,128)}, u32[]{:S(2)}) copy-start(f32[32,32,3,3]{1,0,3,2:T(8,128)} %param.27) | copy-start | bytes 110596
  387.8 193.7 %copy-start.11 = (f32[32]{0:T(128)S(1)}, f32[32]{0:T(128)}, u32[]{:S(2)}) copy-start(f32[32]{0:T(128)} %param.28) | copy-start | bytes 388
  387.8 195.4 %copy-start.9 = (f32[1,32,64]{2,1,0:T(8,128)S(1)}, f32[1,32,64]{2,1,0:T(8,128)}, u32[]{:S(2)}) copy-start(f32[1,32,64]{2,1,0:T(8,128)} %param.29) | copy-start | bytes 24580
  388.9 25.6 %collective-permute-start = (f32[1024,256]{0,1:T(8,128)}, f32[1024,256]{0,1:T(8,128)}, u32[]{:S(2)}, u32[]{:S(2)}) collective-permute-start(f32[1024,256]{0,1:T(8,128)} %constant_dynamic-slice_fusion), channel_id=1, source_target_pairs={{0,64},{16,80},{32,96},{48,112},{64,0},{80,16},{96,32},{112,48},{1... | collective-permute-start | bytes 3145736 | tf_op jit(solution)/shard_map/ppermute | solution.py:14
Sparse Core Ops, SparseCore 0:
  10.5 80.0 all-gather.2
  128.2 156.6 reduce-scatter.1
  288.0 75.4 all-gather.4
  455.0 125.3 all-reduce.2
where the time goes:
time: 591 us; the launch traced here: 590 us
  waiting for transfers between devices  405 us (69%)
  blocking collectives  66.8 us (11%)
  other arithmetic  48.6 us (8%)
  matrix products  46.2 us (8%)
  between operations  14 us (2%)
  local copies, waits for them, and re-layouts  9.16 us (2%)
    reduce_scatter x1, waiting for transfers between devices, body(): lax.psum_scatter(jnp.dot(full_hidden, down_weight, preferred_element_type...  156 us
    psum x1, waiting for transfers between devices, body(): lax.psum((mixed_code * factor[:, None]).astype(jnp.bfloat16), 'mp')  92.3 us
    all_gather x1, waiting for transfers between devices, body(): full_out = lax.all_gather(block_out, 'mp', axis=0, tiled=True)  75.9 us
    all_gather x1, waiting for transfers between devices, body(): gathered = lax.all_gather(tokens, 'mp', axis=0, tiled=True)  57.1 us
    pmax x1, blocking collectives, body(): global_peak = lax.pmax(row_peak, 'mp')  33.6 us
    psum x1, blocking collectives, body(): lax.psum((row_total * factor).astype(jnp.bfloat16), 'mp')  33.2 us
    dot_general x1, matrix products, body(): jnp.dot(full_hidden, down_weight, preferred_element_type=jnp.float32)  28.5 us
    select_n x1, other arithmetic, per_image(): picked = jnp.where(chosen, lookup[1], picked)  24.7 us
  transfers between devices with their start and end apart: 5, of which 5 were waited for; matrix products, arithmetic and copies ran while one was open for 5% of the time, Pallas kernels for 0%

commit v1 on v0

--- a/solution.py
+++ b/solution.py
@@ -74,7 +74,9 @@
     block_out = (
         tokens.astype(jnp.float32) + per_image(ffn_gate, own_images) * (summed + down_bias)
     ).astype(jnp.bfloat16)
-    full_out = lax.all_gather(block_out, "mp", axis=0, tiled=True)
+    full_out = jnp.concatenate(
+        lax.all_to_all(jnp.stack([block_out] * lax.axis_size("mp")), "mp", 0, 0), axis=0
+    )
     logits = (
         jnp.dot(
             modulate(full_out.astype(jnp.float32), per_image(ada_head, row_images)),

time: 591 us -> 678 us (1.15)
  waiting for transfers between devices: 405 us -> 464 us
  other arithmetic: 48.6 us -> 67.3 us
  blocking collectives: 66.8 us -> 79.3 us
  matrix products: 46.2 us -> 34.8 us
    all_to_all x0 -> x1, waiting for transfers between devices: none -> 136 us  [body(): lax.all_to_all(jnp.stack([block_out] * lax.axis_size('mp')), 'mp', 0, 0)]
    all_gather x1 -> x0, waiting for transfers between devices: 75.9 us -> none  [body(): full_out = lax.all_gather(block_out, 'mp', axis=0, tiled=True)]
    convert_element_type x0 -> x1, other arithmetic: none -> 15.9 us  [modulate(): (norm_rows(values) * (1.0 + ada_rows[:, 1]) + ada_rows[:, 0]).astype(jnp....]
    pmax x1, blocking collectives: 33.6 us -> 46.1 us  [body(): global_peak = lax.pmax(row_peak, 'mp')]
    dot_general x1, matrix products: 14 us -> 2.66 us  [body(): jnp.dot(modulate(full_out.astype(jnp.float32), per_image(ada_head, row_im...]
  transfers between devices with their start and end apart: 5 -> 5, of which waited for: 5 -> 5; matrix products, arithmetic and copies ran while one was open for 5% -> 4% of each run, Pallas kernels for 0% -> 0%
where the time goes in v1:
time: 678 us; the launch traced here: 677 us
  waiting for transfers between devices  464 us (68%)
  blocking collectives  79.3 us (12%)
  other arithmetic  67.3 us (10%)
  matrix products  34.8 us (5%)
  between operations  14.1 us (2%)
  local copies, waits for them, and re-layouts  12.4 us (2%)
    reduce_scatter x1, waiting for transfers between devices, body(): lax.psum_scatter(jnp.dot(full_hidden, down_weight, preferred_element_type...  156 us
    all_to_all x1, waiting for transfers between devices, body(): lax.all_to_all(jnp.stack([block_out] * lax.axis_size('mp')), 'mp', 0, 0)  136 us
    psum x1, waiting for transfers between devices, body(): lax.psum((mixed_code * factor[:, None]).astype(jnp.bfloat16), 'mp')  92.3 us
    all_gather x1, waiting for transfers between devices, body(): gathered = lax.all_gather(tokens, 'mp', axis=0, tiled=True)  57.1 us
    pmax x1, blocking collectives, body(): global_peak = lax.pmax(row_peak, 'mp')  46.1 us
    psum x1, blocking collectives, body(): lax.psum((row_total * factor).astype(jnp.bfloat16), 'mp')  33.2 us
    dot_general x1, matrix products, body(): jnp.dot(full_hidden, down_weight, preferred_element_type=jnp.float32)  28.5 us
    select_n x1, other arithmetic, per_image(): picked = jnp.where(chosen, lookup[1], picked)  24.7 us
  transfers between devices with their start and end apart: 5, of which 5 were waited for; matrix products, arithmetic and copies ran while one was open for 4% of the time, Pallas kernels for 0%

profile of v1, /device:TPU:0, one launch (start us, length us, event | category | flops | bytes accessed | tf_op | source)
XLA Modules:
  0.0 677.2 jit_solution(7137891148437685837)
XLA Ops:
  7.2 0.7 all-gather.2.cloned.1.call-update
  8.0 0.8 slice_bitcast_fusion.3
  8.8 24.7 %broadcast_select_fusion = (f32[2048,2,2304]{2,0,1:T(8,128)}, f32[2048,2,2304]{2,0,1:T(8,128)}) fusion(f32[2,2304]{1,0:T(2,128)S(1)} %get-tuple-element.9, f32[2,2304]{1,0:T(2,128)S(1)} %get-tuple-element.8, pred[2048]{0:T(1024)(128)(4,1)S(1)} %fusion.63, f32[2,2304]{1,0:T(2,128)S(1)} %get-tuple-element.16, f32[2,2304]{1,0:T(2,128)S(1)} %get-tuple-element.17), kind=kLoop, calls=%fused_computation.19 | loop fusion | flops 18874368 | bytes 75573248 | tf_op jit(solution)/shard_map/jit(_where)/select_n | solution.py:27
  33.4 57.1 %all-gather.2.cloned.1.call-done = bf16[2048,2304]{1,0:T(8,128)(2,1)} async-done(((bf16[128,2304]{1,0:T(8,128)(2,1)}), bf16[2048,2304]{1,0:T(8,128)(2,1)}) %all-gather.2.cloned.1.call-update) | async-done | bytes 9437200 | tf_op jit(solution)/shard_map/all_gather | solution.py:57
  90.6 5.1 convert_reduce_fusion
  95.7 1.2 copy-done.2
  96.9 2.6 fusion.2
  99.6 28.5 %fusion.25 = f32[2048,2304]{1,0:T(8,128)} fusion(bf16[576,2304]{1,0:T(8,128)(2,1)S(1)} %copy-done, bf16[2304,576]{0,1:T(8,128)(2,1)} %param.18, bf16[2048,2304]{1,0:T(8,128)(2,1)} %all-gather.2.cloned.1.call-done, f32[2048,2,2304]{2,0,1:T(8,128)} %get-tuple-element.15, f32[2048]{0:T(1024)S(1)} %add_rsqrt_fusion, f32[2048]{0:T(1024)S(1)} %broadcast_multiply_fusion.1, ...), kind=kOutput, calls=%fused_computation.33 | convolution fusion | flops 10916462592 | bytes 71387392 | tf_op jit(solution)/shard_map/dot_general | solution.py:69
  128.1 0.7 copy-done.7
  128.9 156.1 %reduce-scatter.2.cloned.1.call-done = f32[128,2304]{1,0:T(8,128)} async-done(((f32[2048,2304]{1,0:T(8,128)}), f32[128,2304]{1,0:T(8,128)}) %reduce-scatter.2.cloned.1.call-update) | async-done | bytes 1179664 | tf_op jit(solution)/shard_map/reduce_scatter | solution.py:68
  285.0 1.5 add_convert_fusion
  286.5 4.4 stack.2
  290.9 4.8 all-to-all-start
  295.7 0.2 all-reduce.3.cloned.1.call-start
  296.0 135.7 %all-to-all-done = bf16[16,128,2304]{2,1,0:T(8,128)(2,1)} async-done(((bf16[16,128,2304]{2,1,0:T(8,128)(2,1)}), bf16[16,128,2304]{2,1,0:T(8,128)(2,1)}, u32[]{:S(2)}, u32[]{:S(2)}) %all-to-all-start) | async-done | bytes 9437216 | tf_op jit(solution)/shard_map/all_to_all | solution.py:78
  431.7 5.0 convert_reduce_fusion.1
  436.6 6.3 multiply_reduce_fusion
  443.0 15.9 %fusion.7 = bf16[2048,2304]{1,0:T(8,128)(2,1)S(1)} fusion(f32[2048,2,2304]{2,0,1:T(8,128)} %get-tuple-element.14, bf16[16,128,2304]{2,1,0:T(8,128)(2,1)} %all-to-all-done, f32[2048]{0:T(1024)S(1)} %rsqrt_bitcast_fusion, f32[2048]{0:T(1024)S(1)} %get-tuple-element.12), kind=kLoop, calls=%fused_computation.10 | loop fusion | flops 33030144 | bytes 56639488 | tf_op jit(solution)/shard_map/convert_element_type | solution.py:32
  458.9 2.7 convolution_add_fusion
  461.6 1.3 copy-done.5
  462.9 1.1 constant_dynamic-slice_fusion
  464.0 2.5 copy.17
  466.6 22.3 %collective-permute-done = f32[1024,256]{0,1:T(8,128)} collective-permute-done((f32[1024,256]{0,1:T(8,128)}, f32[1024,256]{0,1:T(8,128)}, u32[]{:S(2)}, u32[]{:S(2)}) %collective-permute-start) | collective-permute-done | bytes 1048608 | tf_op jit(solution)/shard_map/ppermute | solution.py:14
  488.8 3.3 fusion.90
  492.1 46.1 %pmax.7 = f32[1024]{0:T(1024)S(1)} all-reduce(f32[1024]{0:T(1024)S(1)} %get-tuple-element.6), channel_id=1, replica_groups=mesh['dp'=8,'mp'=16] {'mp'}, use_global_device_ids=true, to_apply=%region_6.7 | all-reduce | flops 1024 | bytes 8192 | tf_op jit(solution)/shard_map/pmax | solution.py:100
  538.2 1.4 convert_reduce_fusion.2
  539.6 2.1 fusion.32
  541.7 33.2 %psum.15 = bf16[1024]{0:T(1024)(128)(2,1)S(1)} all-reduce(bf16[1024]{0:T(1024)(128)(2,1)S(1)} %get-tuple-element.4), channel_id=1, replica_groups=mesh['dp'=8,'mp'=16] {'mp'}, use_global_device_ids=true, to_apply=%region_9.10 | all-reduce | flops 1024 | bytes 4096 | tf_op jit(solution)/shard_map/psum | solution.py:103
  574.9 92.3 %all-reduce.3.cloned.1.call-done = bf16[1024,32]{0,1:T(8,128)(2,1)} async-done(((bf16[1024,32]{0,1:T(8,128)(2,1)}), bf16[1024,32]{0,1:T(8,128)(2,1)}) %all-reduce.3.cloned.1.call-update) | async-done | bytes 65552 | tf_op jit(solution)/shard_map/psum | solution.py:104
  667.3 0.9 convert_divide_fusion
  668.1 0.2 copy.20
  670.0 0.6 add.205
  (51 shorter events, 1.9 us)
Async XLA Ops:
  7.2 92.4 %copy-start = (bf16[576,2304]{1,0:T(8,128)(2,1)S(1)}, bf16[576,2304]{1,0:T(8,128)(2,1)}, u32[]{:S(2)}) copy-start(bf16[576,2304]{1,0:T(8,128)(2,1)} %param.20) | copy-start | bytes 7962628
  7.2 83.4 %all-gather.2.cloned.1.call-start = ((), (), s32[]{:S(2)}) async-start(), calls=%async_computation.2 | async-start | bytes 10027008 | tf_op jit(solution)/shard_map/all_gather | solution.py:57
  7.9 277.0 %reduce-scatter.2.cloned.1.call-start = ((), (), s32[]{:S(2)}) async-start(), calls=%async_computation.3 | async-start | bytes 20054016 | tf_op jit(solution)/shard_map/reduce_scatter | solution.py:68
  33.4 66.1 %copy-start.13 = (f32[576]{0:T(1024)S(1)}, f32[576]{0:T(1024)}, u32[]{:S(2)}) copy-start(f32[576]{0:T(1024)} %param.19) | copy-start | bytes 6916
  90.6 6.4 copy-start.2
  128.1 0.7 copy-start.7
  128.1 156.9 %copy-start.4 = (bf16[128,2304]{1,0:T(8,128)(2,1)S(1)}, bf16[128,2304]{1,0:T(8,128)(2,1)}, u32[]{:S(2)}) copy-start(bf16[128,2304]{1,0:T(8,128)(2,1)} %param.15) | copy-start | bytes 1769476
  128.1 156.9 %copy-start.10 = (f32[2304]{0:T(1024)S(1)}, f32[2304]{0:T(1024)}, u32[]{:S(2)}) copy-start(f32[2304]{0:T(1024)} %param.21) | copy-start | bytes 27652
  286.5 4.4 copy-start.3
  290.9 140.7 %all-to-all-start = ((bf16[16,128,2304]{2,1,0:T(8,128)(2,1)}), bf16[16,128,2304]{2,1,0:T(8,128)(2,1)}, u32[]{:S(2)}, u32[]{:S(2)}) async-start(bf16[16,128,2304]{2,1,0:T(8,128)(2,1)} %stack.2), calls=%async_computation.1 | async-start | bytes 18874368 | tf_op jit(solution)/shard_map/all_to_all | solution.py:78
  295.7 371.5 %all-reduce.3.cloned.1.call-start = ((), (), s32[]{:S(2)}) async-start(), calls=%async_computation.4 | async-start | bytes 131072 | tf_op jit(solution)/shard_map/psum | solution.py:104
  442.9 16.0 %copy-start.12 = (bf16[2304,256]{1,0:T(8,128)(2,1)S(1)}, bf16[2304,256]{1,0:T(8,128)(2,1)}, u32[]{:S(2)}) copy-start(bf16[2304,256]{1,0:T(8,128)(2,1)} %param.23) | copy-start | bytes 3538948
  442.9 16.0 %copy-start.14 = (f32[256]{0:T(256)S(1)}, f32[256]{0:T(256)}, u32[]{:S(2)}) copy-start(f32[256]{0:T(256)} %param.24) | copy-start | bytes 3076
  458.9 211.8 %copy-start.1 = (bf16[576,2304]{1,0:T(8,128)(2,1)S(1)}, bf16[576,2304]{1,0:T(8,128)(2,1)}, u32[]{:S(2)}) copy-start(bf16[576,2304]{1,0:T(8,128)(2,1)} %param.20) | copy-start | bytes 7962628
  461.6 1.4 copy-start.5
  462.9 76.6 %copy-start.8 = (bf16[256,32]{0,1:T(8,128)(2,1)S(1)}, bf16[256,32]{0,1:T(8,128)(2,1)}, u32[]{:S(2)}) copy-start(bf16[256,32]{0,1:T(8,128)(2,1)} %param.26) | copy-start | bytes 49156
  462.9 205.4 %copy-start.6 = (f32[32,32,3,3]{1,0,3,2:T(8,128)S(1)}, f32[32,32,3,3]{1,0,3,2:T(8,128)}, u32[]{:S(2)}) copy-start(f32[32,32,3,3]{1,0,3,2:T(8,128)} %param.27) | copy-start | bytes 110596
  462.9 205.4 %copy-start.11 = (f32[32]{0:T(128)S(1)}, f32[32]{0:T(128)}, u32[]{:S(2)}) copy-start(f32[32]{0:T(128)} %param.28) | copy-start | bytes 388
  462.9 207.1 %copy-start.9 = (f32[1,32,64]{2,1,0:T(8,128)S(1)}, f32[1,32,64]{2,1,0:T(8,128)}, u32[]{:S(2)}) copy-start(f32[1,32,64]{2,1,0:T(8,128)} %param.29) | copy-start | bytes 24580
  464.0 24.8 %collective-permute-start = (f32[1024,256]{0,1:T(8,128)}, f32[1024,256]{0,1:T(8,128)}, u32[]{:S(2)}, u32[]{:S(2)}) collective-permute-start(f32[1024,256]{0,1:T(8,128)} %constant_dynamic-slice_fusion), channel_id=1, source_target_pairs={{0,64},{16,80},{32,96},{48,112},{64,0},{80,16},{96,32},{112,48},{1... | collective-permute-start | bytes 3145736 | tf_op jit(solution)/shard_map/ppermute | solution.py:14
Sparse Core Ops, SparseCore 0:
  10.5 80.0 all-gather.1
  128.2 156.6 reduce-scatter.1
  541.8 125.3 all-reduce.2
